TPU v7x, 768 devices: a whole 4x8x12 slice. The times are simulated.
768 devices in a mesh: section: 96 (over z, y_hi, core), tm: 8 (over y_lo, x).
Axes of the slice: x: 4, y: 8 (y_hi: 4, y_lo: 2; y = y_hi * 2 + y_lo), z: 12, core: 2. Of those that a mesh axis runs over, the one named last changes fastest.
Arguments:
- act_in: bfloat16 [96, 1024, 2048], P('section', 'tm'), may hold values from -6 to 6
- grad_in: bfloat16 [96, 1024, 2048], P('section', 'tm'), may hold values from -6 to 6
- saved_inputs: bfloat16 [96, 2, 1024, 2048], P('section', None, 'tm'), may hold values from -6 to 6
- kernels: bfloat16 [96, 2, 31, 2048], P('section'), may hold values from -1 to 1
- norm_gains: bfloat16 [96, 2, 2048], P('section'), may hold values from 0.099609375 to 1.8984375
- forward_lengths: int32 [96], replicated, may hold values from 512 to 1024
- backward_lengths: int32 [96], replicated, may hold values from 512 to 1024
- forward_slots: int32 [96, 2], replicated, may hold values from 0 to 1
- backward_slots: int32 [96, 2], replicated, may hold values from 0 to 1
Outputs:
- act_out: bfloat16 [96, 1024, 2048], P('section', 'tm')
- grad_out: bfloat16 [96, 1024, 2048], P('section', 'tm')
- tap_grad: float32 [96, 2, 31, 2048], P('section')
- gain_grad: float32 [96, 2, 2048], P('section')
All inputs are finite; a program needn't handle non-finite values.
Results may differ from a plain program's by a relative error of at most 0.0063.
Values may be sent and summed in bfloat16 or wider, within the bound.
A program may use at most 32 MiB of HBM per device.

v0:
```python
import jax
import jax.numpy as jnp
from jax import lax
from jax.sharding import PartitionSpec as P

epsilon = 1e-05


def padded(cells, sides, width):
    for axis, dim in sides:
        count = lax.axis_size(axis)
        ends = count - 1
        head = lax.slice_in_dim(cells, 0, width, axis=dim)
        tail = lax.slice_in_dim(cells, cells.shape[dim] - width, cells.shape[dim], axis=dim)
        cells = jnp.concatenate(
            [
                lax.ppermute(tail, axis, [(i, (i + 1) % count) for i in range(ends)]),
                cells,
                lax.ppermute(head, axis, [((i + 1) % count, i) for i in range(ends)]),
            ],
            axis=dim,
        )
    return cells


def shifted(x, axis, by):
    count = lax.axis_size(axis)
    return lax.ppermute(x, axis, [(i, (i + by) % count) for i in range(count)])


def normalized(inputs):
    values = inputs.astype(jnp.float32)
    center = values - jnp.mean(values, axis=-1, keepdims=True)
    inverse = lax.rsqrt(jnp.mean(center * center, axis=-1, keepdims=True) + epsilon)
    return (center * inverse, inverse)


def pick_slot(lookup, slot_id):
    onehot = (jnp.arange(lookup.shape[0], dtype=jnp.int32) == slot_id).astype(jnp.float32)
    return jnp.tensordot(onehot, lookup.astype(jnp.float32), axes=1)


def depthwise(inputs, taps):
    channels = inputs.shape[1]
    result = lax.conv_general_dilated(
        inputs[None],
        taps[:, None, :],
        (1,),
        "VALID",
        dimension_numbers=("NWC", "WIO", "NWC"),
        feature_group_count=channels,
        preferred_element_type=jnp.float32,
    )
    return result[0]


def local(
    act_in,
    grad_in,
    saved_inputs,
    kernels,
    norm_gains,
    forward_lengths,
    backward_lengths,
    forward_slots,
    backward_slots,
):
    section_count = lax.axis_size("section")
    section_idx = lax.axis_index("section")
    frames_dev = act_in.shape[1]
    width = act_in.shape[2]
    tap_count = kernels.shape[2]
    half_width = (tap_count - 1) // 2
    tick_count = saved_inputs.shape[1]
    frame_ids = lax.axis_index("tm") * frames_dev + jnp.arange(frames_dev, dtype=jnp.int32)
    slot_range = jnp.arange(kernels.shape[1], dtype=jnp.int32)
    own_stack = jnp.concatenate([kernels[0], norm_gains[0][:, None, :]], axis=1)
    carried = act_in[0]
    returning = grad_in[0]
    tap_total = jnp.zeros(kernels.shape[1:], jnp.float32)
    gain_total = jnp.zeros(norm_gains.shape[1:], jnp.float32)
    for tick_step in range(tick_count):
        ahead_chosen = pick_slot(own_stack, forward_slots[section_idx, tick_step])
        ahead_len = forward_lengths[(section_idx - tick_step) % section_count]
        back_slot = backward_slots[section_idx, tick_step]
        back_chosen = pick_slot(own_stack, back_slot)
        back_len = backward_lengths[(section_idx + tick_step) % section_count]
        back_kernel = back_chosen[:tap_count]
        back_gain = back_chosen[tap_count]
        normed_ahead = normalized(carried)[0]
        mask_ahead = (frame_ids < ahead_len).astype(jnp.float32)[:, None]
        normed_back, inverse_back = normalized(saved_inputs[0, tick_step])
        mask_back = (frame_ids < back_len).astype(jnp.float32)[:, None]
        masked_pair = jnp.concatenate(
            [
                mask_ahead * ahead_chosen[tap_count] * normed_ahead,
                mask_back * back_gain * normed_back,
            ],
            axis=1,
        ).astype(jnp.bfloat16)
        padded_pair = padded(masked_pair, (("tm", 0),), half_width)
        kernel_pair = jnp.concatenate([ahead_chosen[:tap_count], back_kernel], axis=1).astype(
            jnp.bfloat16
        )
        conv_pair = depthwise(padded_pair, kernel_pair)
        conv_ahead = conv_pair[:, :width]
        conv_back = conv_pair[:, width:]
        outputs = (carried.astype(jnp.float32) + conv_ahead * jax.nn.sigmoid(conv_ahead)).astype(
            jnp.bfloat16
        )
        gate_back = jax.nn.sigmoid(conv_back)
        grad_up = returning.astype(jnp.float32)
        grad_mixed = (grad_up * gate_back * (1.0 + conv_back * (1.0 - gate_back))).astype(
            jnp.bfloat16
        )
        grad_wide = padded(grad_mixed, (("tm", 0),), half_width)
        tap_term = depthwise(padded_pair[:, width:], grad_mixed)
        grad_masked = mask_back * depthwise(grad_wide, back_kernel[::-1].astype(jnp.bfloat16))
        gain_term = jnp.sum(grad_masked * normed_back, axis=0)
        scaled = grad_masked * back_gain
        grad_norm = inverse_back * (
            scaled
            - jnp.mean(scaled, axis=-1, keepdims=True)
            - normed_back * jnp.mean(scaled * normed_back, axis=-1, keepdims=True)
        )
        grad_x = (grad_up + grad_norm).astype(jnp.bfloat16)
        onehot = (slot_range == back_slot).astype(jnp.float32)
        tap_total = tap_total + onehot[:, None, None] * tap_term[None]
        gain_total = gain_total + onehot[:, None] * gain_term[None]
        carried = shifted(outputs, "section", 1)
        returning = shifted(grad_x, "section", -1)
    tap_sum, gain_sum = lax.psum((tap_total, gain_total), "tm")
    return (carried[None], returning[None], tap_sum[None], gain_sum[None])


def solution(mesh):
    in_specs = (
        P("section", "tm", None),
        P("section", "tm", None),
        P("section", None, "tm", None),
        P("section", None, None, None),
        P("section", None, None),
        P(),
        P(),
        P(),
        P(),
    )
    out_specs = (
        P("section", "tm", None),
        P("section", "tm", None),
        P("section", None, None, None),
        P("section", None, None),
    )
    return jax.shard_map(local, mesh=mesh, in_specs=in_specs, out_specs=out_specs, check_vma=False)
```

profile of v0, /device:TPU:16, one launch (start us, length us, event | category | flops | bytes accessed | tf_op | source)
XLA Modules:
  0.0 242.0 jit_solution(83106499785281734)
XLA Ops:
  8.6 1.3 fusion.21
  10.0 1.4 fusion.98
  18.2 3.4 %collective-permute-start = (bf16[15,4096]{1,0:T(8,128)(2,1)}, bf16[15,4096]{1,0:T(8,128)(2,1)S(1)}, u32[]{:S(2)}, u32[]{:S(2)}) collective-permute-start(bf16[15,4096]{1,0:T(8,128)(2,1)} %get-tuple-element.25), channel_id=1, source_target_pairs={{0,1},{1,2},{2,3},{3,4},{4,5},{5,6},{6,7},{8,9},{9,10},{10,11},{11... | collective-permute-start | bytes 368648 | tf_op jit(solution)/shard_map/ppermute | solution.py:17
  29.9 5.0 %rev.7 = bf16[31,2048]{1,0:T(8,128)(2,1)} reverse(bf16[31,2048]{1,0:T(8,128)(2,1)S(1)} %get-tuple-element.31), dimensions={0} | reverse | bytes 253952 | tf_op jit(solution)/shard_map/rev | solution.py:118
  38.2 1.4 pad_maximum_fusion
  39.6 10.5 %fusion.2 = f32[1,128,4096]{2,0,1:T(1,128)S(1)} fusion(bf16[1,158,4096]{2,1,0:T(8,128)(2,1)S(1)} %get-tuple-element.18, bf16[31,1,2048]{2,1,0:T(2,128)(2,1)S(1)} %copy.23, bf16[31,1,2048]{2,1,0:T(2,128)(2,1)S(1)} %copy.22), kind=kOutput, calls=%fused_computation.2 | convolution fusion | flops 33013760 | bytes 3645440 | tf_op jit(solution)/shard_map/conv_general_dilated | solution.py:45
  50.1 1.6 copy.98
  52.6 4.5 %collective-permute-start.6 = (bf16[15,2048]{1,0:T(8,128)(2,1)S(1)}, bf16[15,2048]{1,0:T(8,128)(2,1)S(1)}, u32[]{:S(2)}, u32[]{:S(2)}) collective-permute-start(bf16[15,2048]{1,0:T(8,128)(2,1)S(1)} %get-tuple-element.29), channel_id=1, source_target_pairs={{0,1},{1,2},{2,3},{3,4},{4,5},{5,6},{6,7},{8,9},{9,10},{10,11},{11... | collective-permute-start | bytes 184328 | tf_op jit(solution)/shard_map/ppermute | solution.py:17
  58.5 1.9 collective-permute-start.2
  60.4 2.9 %collective-permute-done.7 = bf16[15,2048]{1,0:T(8,128)(2,1)S(1)} collective-permute-done((bf16[15,2048]{1,0:T(8,128)(2,1)S(1)}, bf16[15,2048]{1,0:T(8,128)(2,1)S(1)}, u32[]{:S(2)}, u32[]{:S(2)}) %collective-permute-start.7) | collective-permute-done | bytes 61472 | tf_op jit(solution)/shard_map/ppermute | solution.py:19
  63.5 5.1 %fusion.12 = f32[1,128,2048]{2,0,1:T(1,128)S(1)} fusion(bf16[1,158,2048]{2,1,0:T(8,128)(2,1)S(1)} %maximum_bitcast_fusion, bf16[31,1,2048]{2,0,1:T(8,128)(2,1)S(1)} %bitcast.222), kind=kOutput, calls=%fused_computation.29 | convolution fusion | flops 16252928 | bytes 1822720 | tf_op jit(solution)/shard_map/conv_general_dilated | solution.py:45
  71.5 3.9 %collective-permute-start.3 = (bf16[15,4096]{1,0:T(8,128)(2,1)S(1)}, bf16[15,4096]{1,0:T(8,128)(2,1)S(1)}, u32[]{:S(2)}, u32[]{:S(2)}) collective-permute-start(bf16[15,4096]{1,0:T(8,128)(2,1)S(1)} %get-tuple-element.23), channel_id=1, source_target_pairs={{0,1},{1,2},{2,3},{3,4},{4,5},{5,6},{6,7},{8,9},{9,10},{10,11},{11... | collective-permute-start | bytes 368648 | tf_op jit(solution)/shard_map/ppermute | solution.py:17
  75.4 1.5 collective-permute-start.4
  76.9 4.8 %fusion.8 = f32[1,31,2048]{2,0,1:T(1,128)S(1)} fusion(bf16[1,158,2048]{2,1,0:T(8,128)(2,1)S(1)} %slice_bitcast_fusion.1, bf16[128,1,2048]{2,0,1:T(8,128)(2,1)S(1)} %bitcast.200), kind=kOutput, calls=%fused_computation.25 | convolution fusion | flops 16252928 | bytes 1425408 | tf_op jit(solution)/shard_map/conv_general_dilated | solution.py:45
  81.9 2.2 collective-permute-start.8
  84.5 10.5 %fusion = f32[1,128,4096]{2,0,1:T(1,128)S(1)} fusion(bf16[1,158,4096]{2,1,0:T(8,128)(2,1)S(1)} %get-tuple-element.20, bf16[31,1,2048]{2,1,0:T(2,128)(2,1)S(1)} %copy-done.4, bf16[31,1,2048]{2,1,0:T(2,128)(2,1)S(1)} %copy-done.5), kind=kOutput, calls=%fused_computation | convolution fusion | flops 33013760 | bytes 3645440 | tf_op jit(solution)/shard_map/conv_general_dilated | solution.py:45
  95.0 1.6 copy.97
  97.5 4.7 %collective-permute-start.9 = (bf16[15,2048]{1,0:T(8,128)(2,1)S(1)}, bf16[15,2048]{1,0:T(8,128)(2,1)S(1)}, u32[]{:S(2)}, u32[]{:S(2)}) collective-permute-start(bf16[15,2048]{1,0:T(8,128)(2,1)S(1)} %get-tuple-element.27), channel_id=1, source_target_pairs={{0,1},{1,2},{2,3},{3,4},{4,5},{5,6},{6,7},{8,9},{9,10},{10,11},{11... | collective-permute-start | bytes 184328 | tf_op jit(solution)/shard_map/ppermute | solution.py:17
  103.5 4.8 %fusion.6 = f32[1,31,2048]{2,0,1:T(1,128)S(1)} fusion(bf16[1,158,2048]{2,1,0:T(8,128)(2,1)S(1)} %slice_bitcast_fusion, bf16[128,1,2048]{2,0,1:T(8,128)(2,1)S(1)} %bitcast.201), kind=kOutput, calls=%fused_computation.23 | convolution fusion | flops 16252928 | bytes 1425408 | tf_op jit(solution)/shard_map/conv_general_dilated | solution.py:45
  108.5 11.3 %collective-permute-start.5 = (bf16[128,2048]{1,0:T(8,128)(2,1)S(1)}, bf16[128,2048]{1,0:T(8,128)(2,1)S(1)}, u32[]{:S(2)}, u32[]{:S(2)}) collective-permute-start(bf16[128,2048]{1,0:T(8,128)(2,1)S(1)} %get-tuple-element.14), channel_id=1, source_target_pairs={{0,8},{8,16},{16,24},{24,32},{32,40},{40,48},{48,56},{56,64},{64,7... | collective-permute-start | bytes 1572872 | tf_op jit(solution)/shard_map/ppermute | solution.py:28
  119.9 5.1 %fusion.10 = f32[1,128,2048]{2,0,1:T(1,128)S(1)} fusion(bf16[1,158,2048]{2,1,0:T(8,128)(2,1)S(1)} %maximum_bitcast_fusion.1, bf16[31,1,2048]{2,0,1:T(8,128)(2,1)S(1)} %bitcast.221), kind=kOutput, calls=%fused_computation.27 | convolution fusion | flops 16252928 | bytes 1822720 | tf_op jit(solution)/shard_map/conv_general_dilated | solution.py:45
  126.5 10.1 %collective-permute-start.11 = (bf16[128,2048]{1,0:T(8,128)(2,1)S(1)}, bf16[128,2048]{1,0:T(8,128)(2,1)S(1)}, u32[]{:S(2)}, u32[]{:S(2)}) collective-permute-start(bf16[128,2048]{1,0:T(8,128)(2,1)S(1)} %fusion.53), channel_id=1, source_target_pairs={{0,760},{8,0},{16,8},{24,16},{32,24},{40,32},{48,40},{56,48},{64,5... | collective-permute-start | bytes 1572872 | tf_op jit(solution)/shard_map/ppermute | solution.py:28
  137.9 38.0 %psum.15 = f32[1,2,2048]{2,1,0:T(2,128)} all-reduce(f32[1,2,2048]{2,1,0:T(2,128)S(1)} %add_bitcast_fusion.1), channel_id=1, replica_groups=mesh['section'=96,'tm'=8] {'tm'}, use_global_device_ids=true, to_apply=%region_15.16 | all-reduce | flops 4096 | bytes 32768 | tf_op jit(solution)/shard_map/psum | solution.py:132
  176.0 56.8 %all-reduce.2.cloned.1.call-done = f32[1,2,31,2048]{3,1,2,0:T(2,128)} async-done(((f32[1,2,31,2048]{3,1,2,0:T(2,128)}), f32[1,2,31,2048]{3,1,2,0:T(2,128)}) %all-reduce.2.cloned.1.call-update) | async-done | bytes 507920 | tf_op jit(solution)/shard_map/psum | solution.py:132
  (131 shorter events, 32.6 us)
Async XLA Ops:
  7.2 5.5 %copy-start = (bf16[1,2,128,2048]{3,2,1,0:T(8,128)(2,1)S(1)}, bf16[1,2,128,2048]{3,2,1,0:T(8,128)(2,1)}, u32[]{:S(2)}) copy-start(bf16[1,2,128,2048]{3,2,1,0:T(8,128)(2,1)} %param.11) | copy-start | bytes 3145732
  7.2 225.6 %all-reduce.2.cloned.1.call-start = ((), (), s32[]{:S(2)}) async-start(), calls=%async_computation | async-start | bytes 1015808 | tf_op jit(solution)/shard_map/psum | solution.py:132
  7.3 5.9 %copy-start.6 = (bf16[1,2,31,2048]{3,1,2,0:T(2,128)(2,1)S(1)}, bf16[1,2,31,2048]{3,1,2,0:T(2,128)(2,1)}, u32[]{:S(2)}) copy-start(bf16[1,2,31,2048]{3,1,2,0:T(2,128)(2,1)} %param.12) | copy-start | bytes 761860
  7.3 5.9 %copy-start.9 = (bf16[1,2,2048]{2,1,0:T(2,128)(2,1)S(1)}, bf16[1,2,2048]{2,1,0:T(2,128)(2,1)}, u32[]{:S(2)}) copy-start(bf16[1,2,2048]{2,1,0:T(2,128)(2,1)} %param.13) | copy-start | bytes 24580
  12.0 5.0 %copy-start.13 = (f32[128]{0:T(128)}, f32[128]{0:T(128)S(1)}, u32[]{:S(2)}) copy-start(f32[128]{0:T(128)S(1)} %compare_convert_fusion.2) | copy-start | bytes 1540
  18.2 20.0 %collective-permute-start = (bf16[15,4096]{1,0:T(8,128)(2,1)}, bf16[15,4096]{1,0:T(8,128)(2,1)S(1)}, u32[]{:S(2)}, u32[]{:S(2)}) collective-permute-start(bf16[15,4096]{1,0:T(8,128)(2,1)} %get-tuple-element.25), channel_id=1, source_target_pairs={{0,1},{1,2},{2,3},{3,4},{4,5},{5,6},{6,7},{8,9},{9,10},{10,11},{11... | collective-permute-start | bytes 368648 | tf_op jit(solution)/shard_map/ppermute | solution.py:17
  21.6 16.6 %collective-permute-start.1 = (bf16[15,4096]{1,0:T(8,128)(2,1)}, bf16[15,4096]{1,0:T(8,128)(2,1)}, u32[]{:S(2)}, u32[]{:S(2)}) collective-permute-start(bf16[15,4096]{1,0:T(8,128)(2,1)} %get-tuple-element.26), channel_id=1, source_target_pairs={{1,0},{2,1},{3,2},{4,3},{5,4},{6,5},{7,6},{9,8},{10,9},{11,10},{12... | collective-permute-start | bytes 368648 | tf_op jit(solution)/shard_map/ppermute | solution.py:19
  52.6 7.8 %collective-permute-start.6 = (bf16[15,2048]{1,0:T(8,128)(2,1)S(1)}, bf16[15,2048]{1,0:T(8,128)(2,1)S(1)}, u32[]{:S(2)}, u32[]{:S(2)}) collective-permute-start(bf16[15,2048]{1,0:T(8,128)(2,1)S(1)} %get-tuple-element.29), channel_id=1, source_target_pairs={{0,1},{1,2},{2,3},{3,4},{4,5},{5,6},{6,7},{8,9},{9,10},{10,11},{11... | collective-permute-start | bytes 184328 | tf_op jit(solution)/shard_map/ppermute | solution.py:17
  57.1 6.2 %collective-permute-start.7 = (bf16[15,2048]{1,0:T(8,128)(2,1)S(1)}, bf16[15,2048]{1,0:T(8,128)(2,1)S(1)}, u32[]{:S(2)}, u32[]{:S(2)}) collective-permute-start(bf16[15,2048]{1,0:T(8,128)(2,1)S(1)} %get-tuple-element.30), channel_id=1, source_target_pairs={{1,0},{2,1},{3,2},{4,3},{5,4},{6,5},{7,6},{9,8},{10,9},{11,10},{12... | collective-permute-start | bytes 184328 | tf_op jit(solution)/shard_map/ppermute | solution.py:19
  58.5 12.1 %collective-permute-start.2 = (bf16[128,2048]{1,0:T(8,128)(2,1)S(1)}, bf16[128,2048]{1,0:T(8,128)(2,1)S(1)}, u32[]{:S(2)}, u32[]{:S(2)}) collective-permute-start(bf16[128,2048]{1,0:T(8,128)(2,1)S(1)} %get-tuple-element.16), channel_id=1, source_target_pairs={{0,8},{8,16},{16,24},{24,32},{32,40},{40,48},{48,56},{56,64},{64,7... | collective-permute-start | bytes 1572872 | tf_op jit(solution)/shard_map/ppermute | solution.py:28
  63.5 5.2 %copy-start.10 = (f32[128]{0:T(128)S(1)}, f32[128]{0:T(128)}, u32[]{:S(2)}) copy-start(f32[128]{0:T(128)} %broadcast_multiply_fusion.4) | copy-start | bytes 1540
  63.5 5.2 %copy-start.12 = (f32[128]{0:T(128)S(1)}, f32[128]{0:T(128)}, u32[]{:S(2)}) copy-start(f32[128]{0:T(128)} %copy-done.11) | copy-start | bytes 1540
  63.5 5.2 %copy-start.14 = (f32[128]{0:T(128)S(1)}, f32[128]{0:T(128)}, u32[]{:S(2)}) copy-start(f32[128]{0:T(128)} %copy-done.13) | copy-start | bytes 1540
  63.5 5.2 %copy-start.16 = (f32[128]{0:T(128)S(1)}, f32[128]{0:T(128)}, u32[]{:S(2)}) copy-start(f32[128]{0:T(128)} %copy-done.15) | copy-start | bytes 1540
  71.5 12.5 %collective-permute-start.3 = (bf16[15,4096]{1,0:T(8,128)(2,1)S(1)}, bf16[15,4096]{1,0:T(8,128)(2,1)S(1)}, u32[]{:S(2)}, u32[]{:S(2)}) collective-permute-start(bf16[15,4096]{1,0:T(8,128)(2,1)S(1)} %get-tuple-element.23), channel_id=1, source_target_pairs={{0,1},{1,2},{2,3},{3,4},{4,5},{5,6},{6,7},{8,9},{9,10},{10,11},{11... | collective-permute-start | bytes 368648 | tf_op jit(solution)/shard_map/ppermute | solution.py:17
  75.4 8.6 %collective-permute-start.4 = (bf16[15,4096]{1,0:T(8,128)(2,1)S(1)}, bf16[15,4096]{1,0:T(8,128)(2,1)S(1)}, u32[]{:S(2)}, u32[]{:S(2)}) collective-permute-start(bf16[15,4096]{1,0:T(8,128)(2,1)S(1)} %get-tuple-element.24), channel_id=1, source_target_pairs={{1,0},{2,1},{3,2},{4,3},{5,4},{6,5},{7,6},{9,8},{10,9},{11,10},{12... | collective-permute-start | bytes 368648 | tf_op jit(solution)/shard_map/ppermute | solution.py:19
  81.9 14.9 %collective-permute-start.8 = (bf16[128,2048]{1,0:T(8,128)(2,1)S(1)}, bf16[128,2048]{1,0:T(8,128)(2,1)S(1)}, u32[]{:S(2)}, u32[]{:S(2)}) collective-permute-start(bf16[128,2048]{1,0:T(8,128)(2,1)S(1)} %get-tuple-element.21), channel_id=1, source_target_pairs={{0,760},{8,0},{16,8},{24,16},{32,24},{40,32},{48,40},{56,48},{64,5... | collective-permute-start | bytes 1572872 | tf_op jit(solution)/shard_map/ppermute | solution.py:28
  97.5 22.2 %collective-permute-start.9 = (bf16[15,2048]{1,0:T(8,128)(2,1)S(1)}, bf16[15,2048]{1,0:T(8,128)(2,1)S(1)}, u32[]{:S(2)}, u32[]{:S(2)}) collective-permute-start(bf16[15,2048]{1,0:T(8,128)(2,1)S(1)} %get-tuple-element.27), channel_id=1, source_target_pairs={{0,1},{1,2},{2,3},{3,4},{4,5},{5,6},{6,7},{8,9},{9,10},{10,11},{11... | collective-permute-start | bytes 184328 | tf_op jit(solution)/shard_map/ppermute | solution.py:17
  102.2 17.5 %collective-permute-start.10 = (bf16[15,2048]{1,0:T(8,128)(2,1)S(1)}, bf16[15,2048]{1,0:T(8,128)(2,1)S(1)}, u32[]{:S(2)}, u32[]{:S(2)}) collective-permute-start(bf16[15,2048]{1,0:T(8,128)(2,1)S(1)} %get-tuple-element.28), channel_id=1, source_target_pairs={{1,0},{2,1},{3,2},{4,3},{5,4},{6,5},{7,6},{9,8},{10,9},{11,10},{12... | collective-permute-start | bytes 184328 | tf_op jit(solution)/shard_map/ppermute | solution.py:19
  108.4 11.6 %copy-start.7 = (bf16[31,2048]{1,0:T(8,128)(2,1)S(1)}, bf16[31,2048]{1,0:T(8,128)(2,1)}, u32[]{:S(2)}) copy-start(bf16[31,2048]{1,0:T(8,128)(2,1)} %rev.7) | copy-start | bytes 380932
  108.5 67.5 %collective-permute-start.5 = (bf16[128,2048]{1,0:T(8,128)(2,1)S(1)}, bf16[128,2048]{1,0:T(8,128)(2,1)S(1)}, u32[]{:S(2)}, u32[]{:S(2)}) collective-permute-start(bf16[128,2048]{1,0:T(8,128)(2,1)S(1)} %get-tuple-element.14), channel_id=1, source_target_pairs={{0,8},{8,16},{16,24},{24,32},{32,40},{40,48},{48,56},{56,64},{64,7... | collective-permute-start | bytes 1572872 | tf_op jit(solution)/shard_map/ppermute | solution.py:28
  125.8 10.8 %copy-start.17 = (f32[2]{0:T(128)S(1)}, f32[2]{0:T(128)}, u32[]{:S(2)}) copy-start(f32[2]{0:T(128)} %compare_convert_fusion.5) | copy-start | bytes 28
  125.8 10.8 %copy-start.18 = (f32[2]{0:T(128)S(1)}, f32[2]{0:T(128)}, u32[]{:S(2)}) copy-start(f32[2]{0:T(128)} %compare_convert_fusion.4) | copy-start | bytes 28
  126.5 49.4 %collective-permute-start.11 = (bf16[128,2048]{1,0:T(8,128)(2,1)S(1)}, bf16[128,2048]{1,0:T(8,128)(2,1)S(1)}, u32[]{:S(2)}, u32[]{:S(2)}) collective-permute-start(bf16[128,2048]{1,0:T(8,128)(2,1)S(1)} %fusion.53), channel_id=1, source_target_pairs={{0,760},{8,0},{16,8},{24,16},{32,24},{40,32},{48,40},{56,48},{64,5... | collective-permute-start | bytes 1572872 | tf_op jit(solution)/shard_map/ppermute | solution.py:28
  (11 other events, 32.1 us)
Sparse Core Ops, SparseCore 0:
  138.0 94.7 all-reduce.1
where the time goes:
time: 243 us; the launch traced here: 242 us
  waiting for transfers between devices  59.7 us (25%)
  starting transfers between devices  47.4 us (20%)
  matrix products  45.1 us (19%)
  blocking collectives  38 us (16%)
  other arithmetic  20 us (8%)
  local copies, waits for them, and re-layouts  16.7 us (7%)
  between operations  15 us (6%)
    psum x1, waiting for transfers between devices, local(): tap_sum, gain_sum = lax.psum((tap_total, gain_total), 'tm')  56.8 us
    conv_general_dilated x6, matrix products, depthwise(): lax.conv_general_dilated(inputs[None], taps[:, None, :], (1,), 'VALID', d...  40.9 us
    psum x1, blocking collectives, local(): tap_sum, gain_sum = lax.psum((tap_total, gain_total), 'tm')  38 us
    ppermute x4, starting transfers between devices, shifted(): return lax.ppermute(x, axis, [(i, (i + by) % count) for i in range(count)])  25.4 us
    ppermute x4, starting transfers between devices, padded(): lax.ppermute(tail, axis, [(i, (i + 1) % count) for i in range(ends)])  16.6 us
    unnamed x51, local copies, waits for them, and re-layouts  5.92 us
    rev x2, local copies, waits for them, and re-layouts, local(): back_kernel[::-1].astype(jnp.bfloat16)  5.47 us
    ppermute x4, starting transfers between devices, padded(): lax.ppermute(head, axis, [((i + 1) % count, i) for i in range(ends)])  5.35 us
  transfers between devices with their start and end apart: 13, of which 2 were waited for; matrix products, arithmetic and copies ran while one was open for 22% of the time, Pallas kernels for 0%

commit v1 on v0

v1 whole, which is shorter than its diff:
```python
import functools

import jax
import jax.numpy as jnp
from jax import lax
from jax.experimental import pallas as pl
from jax.experimental.pallas import tpu as pltpu
from jax.sharding import PartitionSpec as P

epsilon = 1e-05
MESH = pl.DeviceIdType.MESH
f32 = jnp.float32
bf16 = jnp.bfloat16
LANES = 128
PAD = 16


def row(ref, use, j, c):
    return jnp.broadcast_to(ref[use, pl.ds(j, 1), pl.ds(pl.multiple_of(c * LANES, LANES), LANES)], (8, LANES))


def conv_block(m_ref, k_ref, use, c, groups, flip):
    total = [None] * groups
    for b in range(8):
        taps = {}
        for a in range(4):
            o = 8 * a + b
            if o > 0:
                taps[a] = row(k_ref, use, 31 - o if flip else o - 1, c)
        for i in range(groups + 3):
            cells = m_ref[c, pl.ds(8 * i + b, 8), :]
            for a, tap in taps.items():
                r = i - a
                if 0 <= r < groups:
                    total[r] = tap * cells if total[r] is None else total[r] + tap * cells
    return total


def tap_block(m_ref, gm_ref, tap_ref, tick, c, groups):
    grads = [gm_ref[c, pl.ds(PAD + 8 * r, 8), :] for r in range(groups)]
    lanes = pl.ds(pl.multiple_of(c * LANES, LANES), LANES)
    for b in range(8):
        total = {}
        for i in range(groups + 3):
            cells = m_ref[c, pl.ds(8 * i + b, 8), :]
            for a in range(4):
                r = i - a
                if 8 * a + b > 0 and 0 <= r < groups:
                    total[a] = grads[r] * cells + total[a] if a in total else grads[r] * cells
        for a, value in total.items():
            tap_ref[tick, pl.ds(8 * a + b - 1, 1), lanes] = jnp.sum(value, axis=0, keepdims=True)


def body(
    sections,
    shards,
    act,
    grad,
    saved,
    ksel,
    flen,
    blen,
    act_out,
    grad_out,
    fin,
    x_f,
    x_b,
    g_in,
    k_ref,
    hx,
    m_f,
    m_b,
    gm,
    dref,
    scaled,
    mean_ref,
    inv_ref,
    a_ref,
    b_ref,
    y,
    gx,
    arrive_f,
    arrive_g,
    edge_f,
    gh_send,
    gh_recv,
    tap_ref,
    rs_buf,
    red,
    local_sem,
    hx_s,
    hx_r,
    y_s,
    y_r,
    e_s,
    e_r,
    g_s,
    g_r,
    gh_s,
    gh_r,
    rs_s,
    rs_r,
    ag_s,
    ag_r,
):
    s = lax.axis_index("section")
    t = lax.axis_index("tm")
    rows, width = act.shape
    blocks = width // LANES
    groups = rows // 8
    own = width // shards
    quarter = width // 4
    quarter_blocks = blocks // 4
    after, before = lax.rem(s + 1, sections), lax.rem(s + sections - 1, sections)
    right, left = lax.rem(t + 1, shards), lax.rem(t + shards - 1, shards)
    base = t * rows

    barrier = pltpu.get_barrier_semaphore()
    peers = [(after, t), (before, t), (after, left), (after, right), (before, left), (before, right)]
    peers += [(s, lax.rem(t + d, shards)) for d in range(1, shards)]
    for peer in peers:
        pl.semaphore_signal(barrier, inc=1, device_id=peer, device_id_type=MESH)

    def local(src, dst, n):
        return pltpu.make_async_copy(src, dst, local_sem.at[n])

    loads = [
        local(act, x_f, 0),
        local(ksel, k_ref, 1),
        local(saved.at[0], x_b.at[0], 2),
        local(saved.at[1], x_b.at[1], 3),
        local(grad, g_in, 4),
    ]
    for copy in loads:
        copy.start()

    sent = []

    def remote(src, dst, send, recv, peer):
        return pltpu.make_async_remote_copy(
            src_ref=src, dst_ref=dst, send_sem=send, recv_sem=recv, device_id=peer, device_id_type=MESH
        )

    def launch(copy):
        copy.start()
        sent.append(copy)
        return copy

    def lanes_of(c):
        return pl.ds(pl.multiple_of(c * LANES, LANES), LANES)

    def normalize(load, frame, length, use, m_ref, at, keep=None):
        cells = [load(c) for c in range(blocks)]
        total = cells[0]
        for c in range(1, blocks):
            total = total + cells[c]
        mean = jnp.sum(total, axis=1, keepdims=True) * (1.0 / width)
        cells = [v - mean for v in cells]
        total = cells[0] * cells[0]
        for c in range(1, blocks):
            total = total + cells[c] * cells[c]
        var = jnp.sum(total, axis=1, keepdims=True) * (1.0 / width)
        inverse = lax.rsqrt(var + epsilon)
        ids = frame + lax.broadcasted_iota(jnp.int32, (16, LANES), 0)
        mask = jnp.where((ids >= 0) & (ids < length), 1.0, 0.0).astype(f32)
        scale = mask * inverse
        for c in range(blocks):
            gain = row(k_ref, use, 31, c)
            m_ref[c, pl.ds(at, 16), :] = cells[c] * scale * jnp.concatenate([gain, gain], axis=0)
        if keep is not None:
            mean_ref[keep, pl.ds(at - PAD, 16), :] = jnp.broadcast_to(mean, (16, LANES))
            inv_ref[keep, pl.ds(at - PAD, 16), :] = jnp.broadcast_to(inverse, (16, LANES))

    def norm_own(x_ref, length, use, m_ref, keep=None):
        @pl.loop(0, rows // 16)
        def _(i):
            r = pl.multiple_of(i * 16, 16)
            normalize(
                lambda c: x_ref[pl.ds(r, 16), pl.ds(c * LANES, LANES)].astype(f32),
                base + r,
                length,
                use,
                m_ref,
                pl.multiple_of(PAD + r, 16),
                keep,
            )

    def norm_edges(h_ref, length, use, m_ref):
        @pl.loop(0, 2)
        def _(side):
            normalize(
                lambda c: h_ref[side, :, pl.ds(c * LANES, LANES)].astype(f32),
                base - PAD + side * (rows + PAD),
                length,
                use,
                m_ref,
                pl.multiple_of(side * (rows + PAD), 16),
            )

    f_len = [flen[lax.rem(s + sections - k, sections)] for k in range(2)]
    b_len = [blen[lax.rem(s + k, sections)] for k in range(2)]

    loads[0].wait()
    loads[1].wait()
    norm_own(x_f, f_len[0], 0, m_f)
    pl.semaphore_wait(barrier, len(peers))

    halos = []
    for n, ref in ((0, act), (1, saved.at[0]), (2, saved.at[1])):
        pair = []
        for side, peer in ((1, left), (0, right)):
            edge = pl.ds(0, 16) if side == 1 else pl.ds(rows - 16, 16)
            pair.append(launch(remote(ref.at[edge], hx.at[n, side], hx_s.at[n, side], hx_r.at[n, side], (s, peer))))
        halos.append(pair)

    loads[2].wait()
    norm_own(x_b.at[0], b_len[0], 2, m_b.at[0], 0)
    loads[3].wait()
    norm_own(x_b.at[1], b_len[1], 3, m_b.at[1], 1)

    def forward(tick, x_ref, dst):
        copies = [
            remote(
                y.at[tick, :, pl.ds(q * quarter, quarter)],
                dst.at[:, pl.ds(q * quarter, quarter)],
                y_s.at[tick, q],
                y_r.at[tick, q],
                (after, t),
            )
            for q in range(4)
        ]

        @pl.loop(0, blocks)
        def _(c):
            total = conv_block(m_f, k_ref, tick, c, groups, False)
            for r in range(groups // 2):
                conv = jnp.concatenate(total[2 * r : 2 * r + 2], axis=0)
                x = x_ref[pl.ds(16 * r, 16), lanes_of(c)].astype(f32)
                y[tick, pl.ds(16 * r, 16), lanes_of(c)] = (x + conv * jax.nn.sigmoid(conv)).astype(bf16)
            for q in range(4):

                @pl.when(c == (q + 1) * quarter_blocks - 1)
                def _():
                    copies[q].start()

        sent.extend(copies)
        return copies

    def slope(conv):
        gate = jax.nn.sigmoid(conv)
        return gate * (1.0 + conv * (1.0 - gate))

    def put_mixed(tick, c, r, value):
        gm[c, pl.ds(PAD + 16 * r, 16), :] = value
        if r == 0:
            gh_send[tick, 1, :, lanes_of(c)] = value.astype(bf16)
        if r == groups // 2 - 1:
            gh_send[tick, 0, :, lanes_of(c)] = value.astype(bf16)

    def send_mixed(tick):
        return [
            launch(
                remote(
                    gh_send.at[tick, side],
                    gh_recv.at[tick, side],
                    gh_s.at[tick, side],
                    gh_r.at[tick, side],
                    (s, peer),
                )
            )
            for side, peer in ((1, left), (0, right))
        ]

    def taps(tick):
        @pl.loop(0, blocks)
        def _(c):
            tap_block(m_b.at[tick], gm, tap_ref, tick, c, groups)

    def mixed_edges(tick, copies):
        for copy in copies:
            copy.wait_recv()
        inside = (jnp.where(t > 0, 1.0, 0.0), jnp.where(t < shards - 1, 1.0, 0.0))

        @pl.loop(0, blocks)
        def _(c):
            for side in range(2):
                gm[c, pl.ds(side * (rows + PAD), 16), :] = gh_recv[tick, side, :, lanes_of(c)].astype(f32) * inside[side]

    def normed(tick, r, c):
        x = x_b[tick, pl.ds(r, 16), lanes_of(c)].astype(f32)
        return (x - mean_ref[tick, pl.ds(r, 16), :]) * inv_ref[tick, pl.ds(r, 16), :]

    def input_grad(tick, g_ref, dst):
        use = 2 + tick
        a_ref[...] = jnp.zeros_like(a_ref)
        b_ref[...] = jnp.zeros_like(b_ref)

        @pl.loop(0, blocks)
        def _(c):
            total = conv_block(gm, k_ref, use, c, groups, True)
            gain = row(k_ref, use, 31, c)
            gain = jnp.concatenate([gain, gain], axis=0)
            ids = base + lax.broadcasted_iota(jnp.int32, (16, LANES), 0)
            term = None
            for r in range(groups // 2):
                value = jnp.concatenate(total[2 * r : 2 * r + 2], axis=0)
                value = jnp.where(ids < b_len[tick] - 16 * r, value, 0.0)
                norm = normed(tick, 16 * r, c)
                part = value * norm
                term = part if term is None else term + part
                value = value * gain
                at = pl.ds(16 * r, 16)
                scaled[c, at, :] = value
                a_ref[at, :] += value
                b_ref[at, :] += value * norm
            tap_ref[tick, pl.ds(31, 1), lanes_of(c)] = jnp.sum(term, axis=0, keepdims=True)

        copies = [
            remote(
                gx.at[tick, pl.ds(q * (rows // 4), rows // 4)],
                dst.at[pl.ds(q * (rows // 4), rows // 4)],
                g_s.at[tick, q],
                g_r.at[tick, q],
                (before, t),
            )
            for q in range(4)
        ]

        @pl.loop(0, rows // 16)
        def _(i):
            r = pl.multiple_of(i * 16, 16)
            at = pl.ds(r, 16)
            mean_a = jnp.sum(a_ref[at, :], axis=1, keepdims=True) * (1.0 / width)
            mean_b = jnp.sum(b_ref[at, :], axis=1, keepdims=True) * (1.0 / width)
            inverse = inv_ref[tick, at, :]
            for c in range(blocks):
                lanes = pl.ds(c * LANES, LANES)
                norm = (x_b[tick, at, lanes].astype(f32) - mean_ref[tick, at, :]) * inverse
                value = (scaled[c, at, :] - mean_a - norm * mean_b) * inverse
                gx[tick, at, lanes] = (g_ref[at, lanes].astype(f32) + value).astype(bf16)
            for q in range(4):

                @pl.when(i == (q + 1) * (rows // 64) - 1)
                def _():
                    copies[q].start()

        sent.extend(copies)
        return copies

    def scatter(tick):
        for d in range(1, shards):
            peer = lax.rem(t + d, shards)
            lanes = pl.ds(pl.multiple_of(peer * own, LANES), own)
            launch(
                remote(
                    tap_ref.at[tick, :, lanes],
                    rs_buf.at[tick, t],
                    rs_s.at[tick, d],
                    rs_r.at[tick, t],
                    (s, peer),
                )
            )

    def gather(tick):
        mine = pl.ds(pl.multiple_of(t * own, LANES), own)
        for d in range(1, shards):
            peer = lax.rem(t + d, shards)
            remote(
                tap_ref.at[tick, :, mine], rs_buf.at[tick, peer], rs_s.at[tick, d], rs_r.at[tick, peer], (s, peer)
            ).wait_recv()
        value = tap_ref[tick, :, mine]
        for d in range(1, shards):
            value = value + rs_buf[tick, lax.rem(t + d, shards)]
        red[tick] = value
        keep = local(red.at[tick], fin.at[tick, :, mine], 5 + tick)
        keep.start()
        loads.append(keep)
        for d in range(1, shards):
            launch(
                remote(
                    red.at[tick],
                    fin.at[tick, :, mine],
                    ag_s.at[tick, d],
                    ag_r.at[tick, t],
                    (s, lax.rem(t + d, shards)),
                )
            )

    def gathered(tick):
        for d in range(1, shards):
            peer = lax.rem(t + d, shards)
            theirs = pl.ds(pl.multiple_of(peer * own, LANES), own)
            remote(red.at[tick], fin.at[tick, :, theirs], ag_s.at[tick, d], ag_r.at[tick, peer], (s, peer)).wait_recv()

    for copy in halos[0]:
        copy.wait_recv()
    norm_edges(hx.at[0], f_len[0], 0, m_f)
    ahead = forward(0, x_f, arrive_f)
    edges = []
    for side, peer in ((1, left), (0, right)):
        edge = pl.ds(0, 16) if side == 1 else pl.ds(rows - 16, 16)
        edges.append(launch(remote(y.at[0, edge], edge_f.at[side], e_s.at[side], e_r.at[side], (after, peer))))

    for copy in halos[1]:
        copy.wait_recv()
    norm_edges(hx.at[1], b_len[0], 2, m_b.at[0])
    loads[4].wait()

    @pl.loop(0, blocks)
    def _(c):
        total = conv_block(m_b.at[0], k_ref, 2, c, groups, False)
        for r in range(groups // 2):
            conv = jnp.concatenate(total[2 * r : 2 * r + 2], axis=0)
            put_mixed(0, c, r, g_in[pl.ds(16 * r, 16), lanes_of(c)].astype(f32) * slope(conv))

    mixed = send_mixed(0)
    taps(0)
    mixed_edges(0, mixed)
    behind = input_grad(0, g_in, arrive_g)
    scatter(0)

    for copy in halos[2]:
        copy.wait_recv()
    norm_edges(hx.at[2], b_len[1], 3, m_b.at[1])

    @pl.loop(0, blocks)
    def _(c):
        total = conv_block(m_b.at[1], k_ref, 3, c, groups, False)
        for r in range(groups // 2):
            conv = jnp.concatenate(total[2 * r : 2 * r + 2], axis=0)
            dref[c, pl.ds(16 * r, 16), :] = slope(conv)

    gather(0)

    for copy in ahead + edges:
        copy.wait_recv()
    norm_own(arrive_f, f_len[1], 1, m_f)
    norm_edges(edge_f, f_len[1], 1, m_f)
    ahead = forward(1, arrive_f, act_out)

    for copy in behind:
        copy.wait_recv()

    @pl.loop(0, blocks)
    def _(c):
        for r in range(groups // 2):
            at = pl.ds(16 * r, 16)
            put_mixed(1, c, r, arrive_g[at, lanes_of(c)].astype(f32) * dref[c, at, :])

    mixed = send_mixed(1)
    taps(1)
    mixed_edges(1, mixed)
    behind = input_grad(1, arrive_g, grad_out)
    scatter(1)
    gather(1)
    gathered(0)
    gathered(1)
    for copy in ahead + behind:
        copy.wait_recv()
    for copy in sent:
        copy.wait_send()
    for copy in loads[5:]:
        copy.wait()


def relay(sections, shards, act, grad, saved, ksel, flen, blen):
    rows, width = act.shape
    blocks = width // LANES
    own = width // shards
    vm = pltpu.VMEM
    dma = pltpu.SemaphoreType.DMA
    padded_rows = rows + 2 * PAD
    anywhere = pl.BlockSpec(memory_space=pl.ANY)
    scalars = pl.BlockSpec(memory_space=pltpu.SMEM)
    return pl.pallas_call(
        functools.partial(body, sections, shards),
        out_shape=[
            jax.ShapeDtypeStruct((rows, width), bf16),
            jax.ShapeDtypeStruct((rows, width), bf16),
            jax.ShapeDtypeStruct((2, 32, width), f32),
        ],
        in_specs=[anywhere] * 4 + [scalars] * 2,
        out_specs=[anywhere] * 3,
        scratch_shapes=[
            vm((rows, width), bf16),
            vm((2, rows, width), bf16),
            vm((rows, width), bf16),
            vm((4, 32, width), f32),
            vm((3, 2, 16, width), bf16),
            vm((blocks, padded_rows, LANES), f32),
            vm((2, blocks, padded_rows, LANES), f32),
            vm((blocks, padded_rows, LANES), f32),
            vm((blocks, rows, LANES), f32),
            vm((blocks, rows, LANES), f32),
            vm((2, rows, LANES), f32),
            vm((2, rows, LANES), f32),
            vm((rows, LANES), f32),
            vm((rows, LANES), f32),
            vm((2, rows, width), bf16),
            vm((2, rows, width), bf16),
            vm((rows, width), bf16),
            vm((rows, width), bf16),
            vm((2, 16, width), bf16),
            vm((2, 2, 16, width), bf16),
            vm((2, 2, 16, width), bf16),
            vm((2, 32, width), f32),
            vm((2, shards, 32, own), f32),
            vm((2, 32, own), f32),
            dma((7,)),
            dma((3, 2)),
            dma((3, 2)),
            dma((2, 4)),
            dma((2, 4)),
            dma((2,)),
            dma((2,)),
            dma((2, 4)),
            dma((2, 4)),
            dma((2, 2)),
            dma((2, 2)),
            dma((2, shards)),
            dma((2, shards)),
            dma((2, shards)),
            dma((2, shards)),
        ],
        compiler_params=pltpu.CompilerParams(collective_id=0, has_side_effects=True, vmem_limit_bytes=56 << 20),
        name="relay",
    )(act, grad, saved, ksel, flen, blen)


def local_step(
    act_in,
    grad_in,
    saved_inputs,
    kernels,
    norm_gains,
    forward_lengths,
    backward_lengths,
    forward_slots,
    backward_slots,
):
    sections = lax.axis_size("section")
    shards = lax.axis_size("tm")
    s = lax.axis_index("section")
    stack = jnp.concatenate([kernels[0], norm_gains[0][:, None, :]], axis=1)
    back = backward_slots[s]
    slots = jnp.concatenate([forward_slots[s], back])
    ksel = jnp.where(slots[:, None, None] == 0, stack[0][None], stack[1][None]).astype(f32)
    act_out, grad_out, fin = relay(
        sections, shards, act_in[0], grad_in[0], saved_inputs[0], ksel, forward_lengths, backward_lengths
    )
    onehot = (jnp.arange(kernels.shape[1], dtype=jnp.int32)[:, None] == back[None, :]).astype(f32)
    total = onehot[:, 0, None, None] * fin[0][None] + onehot[:, 1, None, None] * fin[1][None]
    return (act_out[None], grad_out[None], total[None, :, :31], total[None, :, 31])


def solution(mesh):
    in_specs = (
        P("section", "tm", None),
        P("section", "tm", None),
        P("section", None, "tm", None),
        P("section", None, None, None),
        P("section", None, None),
        P(),
        P(),
        P(),
        P(),
    )
    out_specs = (
        P("section", "tm", None),
        P("section", "tm", None),
        P("section", None, None, None),
        P("section", None, None),
    )
    return jax.shard_map(local_step, mesh=mesh, in_specs=in_specs, out_specs=out_specs, check_vma=False)
```

time: 243 us -> 99 us (0.41)
  the two profiles are of different devices: /device:TPU:16 before, /device:TPU:2 now
where the time goes in v1:
time: 99 us; the launch traced here: 98.7 us
  Pallas kernels  89.8 us (91%)
  local copies, waits for them, and re-layouts  6.48 us (7%)
  other arithmetic  1.69 us (2%)
    pallas_call x1, Pallas kernels, relay(): pl.pallas_call(functools.partial(body, sections, shards), out_shape=[jax....  89.8 us
    unnamed x13, local copies, waits for them, and re-layouts  3.76 us

profile of v1, /device:TPU:2, one launch (start us, length us, event | category | flops | bytes accessed | tf_op | source)
XLA Modules:
  0.0 98.7 jit_solution(951463700581895184)
XLA Ops:
  0.6 0.0 copy-start.3
  0.6 0.0 copy-start.4
  0.7 0.7 copy-done.3
  1.3 0.0 copy-done.4
  1.3 0.2 dynamic-slice_reduce_fusion
  1.5 0.1 add_compare_fusion
  1.6 0.0 copy-start.2
  1.6 1.1 %copy.17 = bf16[1,2,31,2048]{3,2,1,0:T(8,128)(2,1)S(1)} copy(bf16[1,2,31,2048]{3,1,2,0:T(2,128)(2,1)} %param.12) | data formatting | bytes 507904 | tf_op args[3]
  2.7 0.0 copy-done.2
  2.8 1.1 %select_convert_fusion.ksel = f32[4,32,2048]{2,1,0:T(8,128)} fusion(pred[4]{0:T(512)(128)(4,1)S(1)} %add_compare_fusion, bf16[32,2048]{1,0:T(8,128)(2,1)S(1)} %get-tuple-element.13, bf16[32,2048]{1,0:T(8,128)(2,1)S(1)} %get-tuple-element.12), kind=kLoop, calls=%fused_computation.1 | loop fusion | flops 524288 | bytes 1310724 | tf_op jit(solution)/shard_map/convert_element_type | solution.py:547
  3.9 89.8 %relay.1 = (bf16[128,2048]{1,0:T(8,128)(2,1)}, bf16[128,2048]{1,0:T(8,128)(2,1)}, f32[2,32,2048]{2,1,0:T(8,128)}) custom-call(bf16[128,2048]{1,0:T(8,128)(2,1)} %bitcast.29, bf16[128,2048]{1,0:T(8,128)(2,1)} %bitcast.30, bf16[2,128,2048]{2,1,0:T(8,128)(2,1)} %bitcast.25, f32[4,32,2048]{2,1,0:T(8,128)} %select_convert_fusion.ksel, s32[96]{0:T(128)} %flen.1, ...), custom_call_target="tpu_custom_call" | custom-call | tf_op jit(solution)/shard_map/relay/pallas_call | solution.py:475
  93.7 1.1 %slice_bitcast_fusion.2 = (f32[32,2048]{1,0:T(8,128)S(1)}, f32[32,2048]{1,0:T(8,128)S(1)}) fusion(f32[2,32,2048]{2,1,0:T(8,128)} %get-tuple-element.9), kind=kLoop, calls=%fused_computation.7 | loop fusion | bytes 1048576 | tf_op jit(solution)/shard_map/mul | solution.py:552
  94.8 0.1 compare_convert_fusion
  94.8 0.4 multiply_add_fusion
  95.2 0.0 copy-start.1
  95.3 0.8 slice_bitcast_fusion
  96.1 0.6 slice_bitcast_fusion.3
  96.7 0.0 copy-done.1
  96.7 0.0 copy-start
  96.7 0.8 copy.20
  97.5 0.4 copy-done
  97.9 0.8 copy.21
  (3 shorter events, 0.1 us)
Async XLA Ops:
  0.6 0.7 copy-start.3
  0.6 0.7 copy-start.4
  1.6 1.1 %copy-start.2 = (bf16[1,2,2048]{2,1,0:T(2,128)(2,1)S(1)}, bf16[1,2,2048]{2,1,0:T(2,128)(2,1)}, u32[]{:S(2)}) copy-start(bf16[1,2,2048]{2,1,0:T(2,128)(2,1)} %param.13) | copy-start | bytes 24580
  95.2 1.4 %copy-start.1 = (bf16[128,2048]{1,0:T(8,128)(2,1)S(1)}, bf16[128,2048]{1,0:T(8,128)(2,1)}, u32[]{:S(2)}) copy-start(bf16[128,2048]{1,0:T(8,128)(2,1)} %get-tuple-element.7) | copy-start | bytes 1572868
  96.7 1.2 %copy-start = (bf16[128,2048]{1,0:T(8,128)(2,1)S(1)}, bf16[128,2048]{1,0:T(8,128)(2,1)}, u32[]{:S(2)}) copy-start(bf16[128,2048]{1,0:T(8,128)(2,1)} %get-tuple-element.8) | copy-start | bytes 1572868

commit v2 on v1

v2 whole, which is shorter than its diff:
```python
import functools

import jax
import jax.numpy as jnp
from jax import lax
from jax.experimental import pallas as pl
from jax.experimental.pallas import tpu as pltpu
from jax.sharding import PartitionSpec as P

epsilon = 1e-05
MESH = pl.DeviceIdType.MESH
f32 = jnp.float32
bf16 = jnp.bfloat16
LANES = 128
PAD = 16


def row(ref, use, j, c):
    return jnp.broadcast_to(ref[use, pl.ds(j, 1), pl.ds(pl.multiple_of(c * LANES, LANES), LANES)], (8, LANES))


def conv_block(m_ref, k_ref, use, c, first, groups, flip):
    total = [None] * groups
    for b in range(8):
        taps = {}
        for a in range(4):
            o = 8 * a + b
            if o > 0:
                taps[a] = row(k_ref, use, 31 - o if flip else o - 1, c)
        for i in range(groups + 3):
            cells = m_ref[c, pl.ds(8 * (first + i) + b, 8), :]
            for a, tap in taps.items():
                r = i - a
                if 0 <= r < groups:
                    total[r] = tap * cells if total[r] is None else total[r] + tap * cells
    return total


def tap_block(m_ref, gm_ref, tap_ref, tick, c, groups):
    grads = [gm_ref[c, pl.ds(PAD + 8 * r, 8), :] for r in range(groups)]
    lanes = pl.ds(pl.multiple_of(c * LANES, LANES), LANES)
    for b in range(8):
        total = {}
        for i in range(groups + 3):
            cells = m_ref[c, pl.ds(8 * i + b, 8), :]
            for a in range(4):
                r = i - a
                if 8 * a + b > 0 and 0 <= r < groups:
                    total[a] = grads[r] * cells + total[a] if a in total else grads[r] * cells
        for a, value in total.items():
            tap_ref[tick, pl.ds(8 * a + b - 1, 1), lanes] = jnp.sum(value, axis=0, keepdims=True)


def body(
    sections,
    shards,
    act,
    grad,
    saved,
    kernels,
    gains,
    flen,
    blen,
    fslot,
    bslot,
    act_out,
    grad_out,
    fin,
    x_f,
    x_b,
    g_in,
    k_raw,
    gain_raw,
    k_ref,
    hx,
    m_f,
    m_b,
    gm,
    dref,
    scaled,
    mean_ref,
    inv_ref,
    a_ref,
    b_ref,
    y,
    gx,
    arrive_f,
    arrive_g,
    edge_f,
    gh_send,
    gh_recv,
    tap_ref,
    tap_bf,
    rs_buf,
    part,
    part_in,
    red,
    local_sem,
    hx_s,
    hx_r,
    y_s,
    y_r,
    e_s,
    e_r,
    g_s,
    g_r,
    gh_s,
    gh_r,
    rs_s,
    rs_r,
    pr_s,
    pr_r,
    ag_s,
    ag_r,
):
    s = lax.axis_index("section")
    t = lax.axis_index("tm")
    rows, width = act.shape
    blocks = width // LANES
    tiles = rows // 16
    quarter = width // 4
    quarter_blocks = blocks // 4
    band = rows // 4
    line = shards // 2
    own = width // line
    t_x, t_y = lax.rem(t, line), lax.div(t, line)
    after, before = lax.rem(s + 1, sections), lax.rem(s + sections - 1, sections)
    right, left = lax.rem(t + 1, shards), lax.rem(t + shards - 1, shards)
    base = t * rows
    outer = ((0, band // 8), (3 * band // 8, band // 8))
    inner = ((band // 8, band // 4),)

    barrier = pltpu.get_barrier_semaphore()
    peers = [(after, t), (before, t), (after, left), (after, right), (before, left), (before, right)]
    peers += [(s, lax.rem(t + d, shards)) for d in range(1, shards)]
    for peer in peers:
        pl.semaphore_signal(barrier, inc=1, device_id=peer, device_id_type=MESH)

    def local(src, dst, n):
        return pltpu.make_async_copy(src, dst, local_sem.at[n])

    loads = [
        local(kernels, k_raw, 0),
        local(gains, gain_raw, 1),
        local(saved.at[0], x_b.at[0], 2),
        local(act, x_f, 3),
        local(saved.at[1], x_b.at[1], 4),
        local(grad, g_in, 5),
    ]
    for copy in loads:
        copy.start()

    sent = []

    def remote(src, dst, send, recv, peer):
        return pltpu.make_async_remote_copy(
            src_ref=src, dst_ref=dst, send_sem=send, recv_sem=recv, device_id=peer, device_id_type=MESH
        )

    def launch(copy):
        copy.start()
        sent.append(copy)
        return copy

    def lanes_of(c):
        return pl.ds(pl.multiple_of(c * LANES, LANES), LANES)

    def twice(value):
        return jnp.concatenate([value, value], axis=0)

    f_len = [flen[lax.rem(s + sections - k, sections)] for k in range(2)]
    b_len = [blen[lax.rem(s + k, sections)] for k in range(2)]
    slots = [fslot[0, s], fslot[1, s], bslot[0, s], bslot[1, s]]

    def pick(use):
        one = slots[use].astype(f32)
        zero = 1.0 - one
        pair = gain_raw[...].astype(f32)
        k_ref[use, pl.ds(31, 1), :] = pair[0:1] * zero + pair[1:2] * one

        for j in range(31):
            pair = k_raw[j].astype(f32)
            k_ref[use, pl.ds(j, 1), :] = pair[0:1] * zero + pair[1:2] * one

    def normalize(load, count, frames, at, length, use, m_ref, keep=None):
        zeros = [jnp.zeros((16, LANES), f32)] * count

        def sums(c, totals):
            return [total + load(n, c) for n, total in enumerate(totals)]

        totals = lax.fori_loop(0, blocks, sums, zeros, unroll=4)
        means = [
            jnp.broadcast_to(jnp.sum(total, axis=1, keepdims=True) * (1.0 / width), (16, LANES)) for total in totals
        ]

        def squares(c, totals):
            out = []
            for n, total in enumerate(totals):
                center = load(n, c) - means[n]
                out.append(total + center * center)
            return out

        totals = lax.fori_loop(0, blocks, squares, zeros, unroll=4)
        scales = []
        for n, total in enumerate(totals):
            var = jnp.sum(total, axis=1, keepdims=True) * (1.0 / width)
            inverse = jnp.broadcast_to(lax.rsqrt(var + epsilon), (16, LANES))
            if keep is not None:
                mean_ref[keep, pl.ds(16 * n, 16), :] = means[n]
                inv_ref[keep, pl.ds(16 * n, 16), :] = inverse
            ids = frames[n] + lax.broadcasted_iota(jnp.int32, (16, LANES), 0)
            scales.append(jnp.where((ids >= 0) & (ids < length), inverse, 0.0))

        def write(c, _):
            gain = twice(row(k_ref, use, 31, c))
            for n in range(count):
                m_ref[c, pl.ds(at[n], 16), :] = (load(n, c) - means[n]) * scales[n] * gain
            return 0

        lax.fori_loop(0, blocks, write, 0, unroll=2)

    def norm_own(x_ref, length, use, m_ref, keep=None):
        normalize(
            lambda n, c: x_ref[pl.ds(16 * n, 16), lanes_of(c)].astype(f32),
            tiles,
            [base + 16 * n for n in range(tiles)],
            [PAD + 16 * n for n in range(tiles)],
            length,
            use,
            m_ref,
            keep,
        )

    def norm_edges(h_ref, length, use, m_ref):
        normalize(
            lambda n, c: h_ref[n, :, lanes_of(c)].astype(f32),
            2,
            [base - PAD, base + rows],
            [0, rows + PAD],
            length,
            use,
            m_ref,
        )

    loads[0].wait()
    loads[1].wait()
    pick(2)
    pl.semaphore_wait(barrier, len(peers))

    halos = {}
    for n, ref in ((1, saved.at[0]), (0, act), (2, saved.at[1])):
        halos[n] = []
        for side, peer in ((1, left), (0, right)):
            edge = pl.ds(0, 16) if side == 1 else pl.ds(rows - 16, 16)
            halos[n].append(
                launch(remote(ref.at[edge], hx.at[n, side], hx_s.at[n, side], hx_r.at[n, side], (s, peer)))
            )

    loads[2].wait()
    norm_own(x_b.at[0], b_len[0], 2, m_b.at[0], 0)
    loads[3].wait()
    pick(0)
    norm_own(x_f, f_len[0], 0, m_f)

    def forward(tick, x_ref, dst):
        copies = [
            remote(
                y.at[tick, :, pl.ds(q * quarter, quarter)],
                dst.at[:, pl.ds(q * quarter, quarter)],
                y_s.at[tick, q],
                y_r.at[tick, q],
                (after, t),
            )
            for q in range(4)
        ]

        @pl.loop(0, blocks)
        def _(c):
            total = conv_block(m_f, k_ref, tick, c, 0, 2 * tiles, False)
            for r in range(tiles):
                conv = jnp.concatenate(total[2 * r : 2 * r + 2], axis=0)
                x = x_ref[pl.ds(16 * r, 16), lanes_of(c)].astype(f32)
                y[tick, pl.ds(16 * r, 16), lanes_of(c)] = (x + conv * jax.nn.sigmoid(conv)).astype(bf16)
            for q in range(4):

                @pl.when(c == (q + 1) * quarter_blocks - 1)
                def _():
                    copies[q].start()

        sent.extend(copies)
        return copies

    def slope(conv):
        gate = jax.nn.sigmoid(conv)
        return gate * (1.0 + conv * (1.0 - gate))

    def put_mixed(tick, c, r, value):
        gm[c, pl.ds(PAD + 16 * r, 16), :] = value
        if r == 0:
            gh_send[tick, 1, :, lanes_of(c)] = value.astype(bf16)
        if r == tiles - 1:
            gh_send[tick, 0, :, lanes_of(c)] = value.astype(bf16)

    def send_mixed(tick):
        return [
            launch(
                remote(
                    gh_send.at[tick, side],
                    gh_recv.at[tick, side],
                    gh_s.at[tick, side],
                    gh_r.at[tick, side],
                    (s, peer),
                )
            )
            for side, peer in ((1, left), (0, right))
        ]

    def taps(tick):
        @pl.loop(0, blocks)
        def _(c):
            tap_block(m_b.at[tick], gm, tap_ref, tick, c, 2 * tiles)

        tap_bf[tick] = tap_ref[tick].astype(bf16)

    def mixed_edges(tick, copies):
        for copy in copies:
            copy.wait_recv()
        inside = (jnp.where(t > 0, 1.0, 0.0), jnp.where(t < shards - 1, 1.0, 0.0))

        @pl.loop(0, blocks)
        def _(c):
            for side in range(2):
                gm[c, pl.ds(side * (rows + PAD), 16), :] = gh_recv[tick, side, :, lanes_of(c)].astype(f32) * inside[side]

    def normed(tick, r, c):
        x = x_b[tick, pl.ds(r, 16), lanes_of(c)].astype(f32)
        return (x - mean_ref[tick, pl.ds(r, 16), :]) * inv_ref[tick, pl.ds(r, 16), :]

    def input_grad(tick, g_ref, dst):
        use = 2 + tick
        a_ref[...] = jnp.zeros_like(a_ref)
        b_ref[...] = jnp.zeros_like(b_ref)
        copies = {}
        for turn, (segments, bands) in enumerate(((outer, (0, 3)), (inner, (1, 2)))):

            @pl.loop(0, blocks)
            def _(c):
                gain = twice(row(k_ref, use, 31, c))
                ids = base + lax.broadcasted_iota(jnp.int32, (16, LANES), 0)
                term = None
                for first, groups in segments:
                    total = conv_block(gm, k_ref, use, c, first, groups, True)
                    for n in range(groups // 2):
                        r = 8 * first + 16 * n
                        value = jnp.concatenate(total[2 * n : 2 * n + 2], axis=0)
                        value = jnp.where(ids < b_len[tick] - r, value, 0.0)
                        norm = normed(tick, r, c)
                        part_term = value * norm
                        term = part_term if term is None else term + part_term
                        value = value * gain
                        at = pl.ds(r, 16)
                        scaled[c, at, :] = value
                        a_ref[at, :] += value
                        b_ref[at, :] += value * norm
                total_term = jnp.sum(term, axis=0, keepdims=True)
                if turn > 0:
                    total_term = total_term + tap_ref[tick, pl.ds(31, 1), lanes_of(c)]
                tap_ref[tick, pl.ds(31, 1), lanes_of(c)] = total_term

            starts = [q * band + 16 * n for q in bands for n in range(band // 16)]
            fixed = []
            for r in starts:
                at = pl.ds(r, 16)
                mean_a = jnp.broadcast_to(jnp.sum(a_ref[at, :], axis=1, keepdims=True) * (1.0 / width), (16, LANES))
                mean_b = jnp.broadcast_to(jnp.sum(b_ref[at, :], axis=1, keepdims=True) * (1.0 / width), (16, LANES))
                fixed.append((mean_a, mean_b))
            for (mean_a, mean_b), r in zip(fixed, starts):
                a_ref[pl.ds(r, 16), :] = mean_a
                b_ref[pl.ds(r, 16), :] = mean_b
            for q in bands:
                mine = [q * band + 16 * n for n in range(band // 16)]
                held = [
                    [ref[pl.ds(r, 16), :] for ref in (a_ref, b_ref, mean_ref.at[tick], inv_ref.at[tick])] for r in mine
                ]

                def write(c, _):
                    for r, (mean_a, mean_b, mean, inverse) in zip(mine, held):
                        at = pl.ds(r, 16)
                        norm = (x_b[tick, at, lanes_of(c)].astype(f32) - mean) * inverse
                        value = (scaled[c, at, :] - mean_a - norm * mean_b) * inverse
                        gx[tick, at, lanes_of(c)] = (g_ref[at, lanes_of(c)].astype(f32) + value).astype(bf16)
                    return 0

                lax.fori_loop(0, blocks, write, 0, unroll=2)
                copies[q] = launch(
                    remote(
                        gx.at[tick, pl.ds(q * band, band)],
                        dst.at[pl.ds(q * band, band)],
                        g_s.at[tick, q],
                        g_r.at[tick, q],
                        (before, t),
                    )
                )
        return copies

    def lane_part(n):
        return pl.ds(pl.multiple_of(n * own, LANES), own)

    def scatter(tick):
        for d in range(1, line):
            peer = lax.rem(t_x + d, line)
            launch(
                remote(
                    tap_bf.at[tick, :, lane_part(peer)],
                    rs_buf.at[tick, t_x],
                    rs_s.at[tick, d],
                    rs_r.at[tick, t_x],
                    (s, t_y * line + peer),
                )
            )

    def exchange(tick):
        value = tap_ref[tick, :, lane_part(t_x)]
        for d in range(1, line):
            peer = lax.rem(t_x + d, line)
            remote(
                tap_bf.at[tick, :, lane_part(peer)],
                rs_buf.at[tick, peer],
                rs_s.at[tick, d],
                rs_r.at[tick, peer],
                (s, t_y * line + peer),
            ).wait_recv()
            value = value + rs_buf[tick, peer].astype(f32)
        part[tick] = value.astype(bf16)
        return launch(
            remote(part.at[tick], part_in.at[tick], pr_s.at[tick], pr_r.at[tick], (s, (1 - t_y) * line + t_x))
        )

    def gather(tick, swap):
        swap.wait_recv()
        red[tick] = (part[tick].astype(f32) + part_in[tick].astype(f32)).astype(bf16)
        keep = local(red.at[tick], fin.at[tick, :, lane_part(t_x)], 6 + tick)
        keep.start()
        loads.append(keep)
        for d in range(1, line):
            launch(
                remote(
                    red.at[tick],
                    fin.at[tick, :, lane_part(t_x)],
                    ag_s.at[tick, d],
                    ag_r.at[tick, t_x],
                    (s, t_y * line + lax.rem(t_x + d, line)),
                )
            )

    def gathered(tick):
        for d in range(1, line):
            peer = lax.rem(t_x + d, line)
            remote(
                red.at[tick],
                fin.at[tick, :, lane_part(peer)],
                ag_s.at[tick, d],
                ag_r.at[tick, peer],
                (s, t_y * line + peer),
            ).wait_recv()

    for copy in halos[1]:
        copy.wait_recv()
    norm_edges(hx.at[1], b_len[0], 2, m_b.at[0])
    loads[5].wait()

    @pl.loop(0, blocks)
    def _(c):
        total = conv_block(m_b.at[0], k_ref, 2, c, 0, 2 * tiles, False)
        for r in range(tiles):
            conv = jnp.concatenate(total[2 * r : 2 * r + 2], axis=0)
            put_mixed(0, c, r, g_in[pl.ds(16 * r, 16), lanes_of(c)].astype(f32) * slope(conv))

    mixed = send_mixed(0)
    for copy in halos[0]:
        copy.wait_recv()
    norm_edges(hx.at[0], f_len[0], 0, m_f)
    ahead = forward(0, x_f, arrive_f)
    edges = []
    for side, peer in ((1, left), (0, right)):
        edge = pl.ds(0, 16) if side == 1 else pl.ds(rows - 16, 16)
        edges.append(launch(remote(y.at[0, edge], edge_f.at[side], e_s.at[side], e_r.at[side], (after, peer))))
    mixed_edges(0, mixed)
    behind = input_grad(0, g_in, arrive_g)
    taps(0)
    scatter(0)

    loads[4].wait()
    pick(3)
    norm_own(x_b.at[1], b_len[1], 3, m_b.at[1], 1)
    for copy in halos[2]:
        copy.wait_recv()
    norm_edges(hx.at[2], b_len[1], 3, m_b.at[1])

    @pl.loop(0, blocks)
    def _(c):
        total = conv_block(m_b.at[1], k_ref, 3, c, 0, 2 * tiles, False)
        for r in range(tiles):
            conv = jnp.concatenate(total[2 * r : 2 * r + 2], axis=0)
            dref[c, pl.ds(16 * r, 16), :] = slope(conv)

    pick(1)
    swap = exchange(0)

    def mix_bands(bands):
        for q in bands:
            behind[q].wait_recv()

        @pl.loop(0, blocks)
        def _(c):
            for q in bands:
                for r in range(q * band // 16, (q + 1) * band // 16):
                    at = pl.ds(16 * r, 16)
                    put_mixed(1, c, r, arrive_g[at, lanes_of(c)].astype(f32) * dref[c, at, :])

    mix_bands((0, 3))
    mixed = send_mixed(1)
    gather(0, swap)
    for copy in ahead + edges:
        copy.wait_recv()
    norm_own(arrive_f, f_len[1], 1, m_f)
    norm_edges(edge_f, f_len[1], 1, m_f)
    ahead = forward(1, arrive_f, act_out)
    mix_bands((1, 2))
    mixed_edges(1, mixed)
    behind = input_grad(1, arrive_g, grad_out)
    taps(1)
    scatter(1)
    swap = exchange(1)
    gather(1, swap)
    gathered(0)
    gathered(1)
    for copy in ahead + list(behind.values()):
        copy.wait_recv()
    for copy in sent:
        copy.wait_send()
    for copy in loads[6:]:
        copy.wait()


def relay(sections, shards, act, grad, saved, kernels, gains, flen, blen, fslot, bslot):
    rows, width = act.shape
    blocks = width // LANES
    line = shards // 2
    own = width // line
    vm = pltpu.VMEM
    dma = pltpu.SemaphoreType.DMA
    padded_rows = rows + 2 * PAD
    anywhere = pl.BlockSpec(memory_space=pl.ANY)
    scalars = pl.BlockSpec(memory_space=pltpu.SMEM)
    return pl.pallas_call(
        functools.partial(body, sections, shards),
        out_shape=[
            jax.ShapeDtypeStruct((rows, width), bf16),
            jax.ShapeDtypeStruct((rows, width), bf16),
            jax.ShapeDtypeStruct((2, 32, width), bf16),
        ],
        in_specs=[anywhere] * 5 + [scalars] * 4,
        out_specs=[anywhere] * 3,
        scratch_shapes=[
            vm((rows, width), bf16),
            vm((2, rows, width), bf16),
            vm((rows, width), bf16),
            vm((31, 2, width), bf16),
            vm((2, width), bf16),
            vm((4, 32, width), f32),
            vm((3, 2, 16, width), bf16),
            vm((blocks, padded_rows, LANES), f32),
            vm((2, blocks, padded_rows, LANES), f32),
            vm((blocks, padded_rows, LANES), f32),
            vm((blocks, rows, LANES), f32),
            vm((blocks, rows, LANES), f32),
            vm((2, rows, LANES), f32),
            vm((2, rows, LANES), f32),
            vm((rows, LANES), f32),
            vm((rows, LANES), f32),
            vm((2, rows, width), bf16),
            vm((2, rows, width), bf16),
            vm((rows, width), bf16),
            vm((rows, width), bf16),
            vm((2, 16, width), bf16),
            vm((2, 2, 16, width), bf16),
            vm((2, 2, 16, width), bf16),
            vm((2, 32, width), f32),
            vm((2, 32, width), bf16),
            vm((2, line, 32, own), bf16),
            vm((2, 32, own), bf16),
            vm((2, 32, own), bf16),
            vm((2, 32, own), bf16),
            dma((8,)),
            dma((3, 2)),
            dma((3, 2)),
            dma((2, 4)),
            dma((2, 4)),
            dma((2,)),
            dma((2,)),
            dma((2, 4)),
            dma((2, 4)),
            dma((2, 2)),
            dma((2, 2)),
            dma((2, line)),
            dma((2, line)),
            dma((2,)),
            dma((2,)),
            dma((2, line)),
            dma((2, line)),
        ],
        compiler_params=pltpu.CompilerParams(collective_id=0, has_side_effects=True, vmem_limit_bytes=56 << 20),
        name="relay",
    )(act, grad, saved, kernels, gains, flen, blen, fslot, bslot)


def finish_body(section, bslot, act, grad, fin, act_out, grad_out, tap_out, gain_out, wide, fin_v, full, taps, gains, sem_in, sem_out):
    rows = act.shape[0]
    half = rows // 2
    moves = []
    for n, (src, dst) in enumerate(((act, act_out), (grad, grad_out))):
        for h in range(2):
            at = pl.ds(h * half, half)
            k = 2 * n + h
            moves.append(
                (
                    pltpu.make_async_copy(src.at[at], wide.at[k], sem_in.at[k]),
                    pltpu.make_async_copy(wide.at[k], dst.at[at], sem_out.at[k]),
                )
            )
    bring = pltpu.make_async_copy(fin, fin_v, sem_in.at[4])
    bring.start()
    for come, _ in moves:
        come.start()
    bring.wait()
    full[...] = fin_v[...].astype(f32)
    slot = lax.broadcasted_iota(jnp.int32, (2, LANES), 0)
    hot = [jnp.where(slot == bslot[k, section[0]], 1.0, 0.0) for k in range(2)]
    blocks = full.shape[2] // LANES

    def one(j, c):
        lanes = pl.ds(c * LANES, LANES)
        return sum(hot[k] * jnp.broadcast_to(full[k, pl.ds(j, 1), lanes], (2, LANES)) for k in range(2))

    for c in range(blocks):
        gains[:, pl.ds(c * LANES, LANES)] = one(31, c)

    for j in range(31):
        for c in range(blocks):
            taps[j, :, pl.ds(c * LANES, LANES)] = one(j, c)

    put = [
        pltpu.make_async_copy(taps, tap_out, sem_out.at[4]),
        pltpu.make_async_copy(gains, gain_out, sem_out.at[5]),
    ]
    for copy in put:
        copy.start()
    for come, go in moves:
        come.wait()
        go.start()
        put.append(go)
    for copy in put:
        copy.wait()


def finish(section, bslot, act, grad, fin):
    rows, width = act.shape
    vm = pltpu.VMEM
    dma = pltpu.SemaphoreType.DMA
    anywhere = pl.BlockSpec(memory_space=pl.ANY)
    scalars = pl.BlockSpec(memory_space=pltpu.SMEM)
    return pl.pallas_call(
        finish_body,
        out_shape=[
            jax.ShapeDtypeStruct((rows, width), bf16),
            jax.ShapeDtypeStruct((rows, width), bf16),
            jax.ShapeDtypeStruct((31, 2, width), f32),
            jax.ShapeDtypeStruct((2, width), f32),
        ],
        in_specs=[scalars] * 2 + [anywhere] * 3,
        out_specs=[anywhere] * 4,
        scratch_shapes=[
            vm((4, rows // 2, width), bf16),
            vm((2, 32, width), bf16),
            vm((2, 32, width), f32),
            vm((31, 2, width), f32),
            vm((2, width), f32),
            dma((5,)),
            dma((6,)),
        ],
        compiler_params=pltpu.CompilerParams(vmem_limit_bytes=56 << 20),
        name="finish",
    )(section, bslot, act, grad, fin)


def local_step(
    act_in,
    grad_in,
    saved_inputs,
    kernels,
    norm_gains,
    forward_lengths,
    backward_lengths,
    forward_slots,
    backward_slots,
):
    sections = lax.axis_size("section")
    shards = lax.axis_size("tm")
    s = lax.axis_index("section")
    act_out, grad_out, fin = relay(
        sections,
        shards,
        act_in[0],
        grad_in[0],
        saved_inputs[0],
        jnp.transpose(kernels[0], (1, 0, 2)),
        norm_gains[0],
        forward_lengths,
        backward_lengths,
        forward_slots.T,
        backward_slots.T,
    )
    act_out, grad_out, taps, gains = finish(s[None].astype(jnp.int32), backward_slots.T, act_out, grad_out, fin)
    return (act_out[None], grad_out[None], jnp.transpose(taps, (1, 0, 2))[None], gains[None])


def solution(mesh):
    in_specs = (
        P("section", "tm", None),
        P("section", "tm", None),
        P("section", None, "tm", None),
        P("section", None, None, None),
        P("section", None, None),
        P(),
        P(),
        P(),
        P(),
    )
    out_specs = (
        P("section", "tm", None),
        P("section", "tm", None),
        P("section", None, None, None),
        P("section", None, None),
    )
    return jax.shard_map(local_step, mesh=mesh, in_specs=in_specs, out_specs=out_specs, check_vma=False)
```

time: 99 us -> 84.1 us (0.85)
  the two profiles are of different devices: /device:TPU:2 before, /device:TPU:4 now
where the time goes in v2:
time: 84.1 us; the launch traced here: 83.9 us
  Pallas kernels  83.3 us (99%)
    pallas_call x1, Pallas kernels, relay(): pl.pallas_call(functools.partial(body, sections, shards), out_shape=[jax....  80.1 us
    pallas_call x1, Pallas kernels, finish(): pl.pallas_call(finish_body, out_shape=[jax.ShapeDtypeStruct((rows, width)...  3.18 us

profile of v2, /device:TPU:4, one launch (start us, length us, event | category | flops | bytes accessed | tf_op | source)
XLA Modules:
  0.0 83.9 jit_solution(6995507010108650225)
XLA Ops:
  0.6 80.1 %relay.1 = (bf16[128,2048]{1,0:T(8,128)(2,1)}, bf16[128,2048]{1,0:T(8,128)(2,1)}, bf16[2,32,2048]{2,1,0:T(8,128)(2,1)}) custom-call(bf16[128,2048]{1,0:T(8,128)(2,1)} %bitcast.17, bf16[128,2048]{1,0:T(8,128)(2,1)} %bitcast.18, bf16[2,128,2048]{2,1,0:T(8,128)(2,1)} %bitcast.16, bf16[31,2,2048]{2,1,0:T(2,128)(2,1)} %bitcast.19, bf16[2,2048]{1,0:T(2,128)(2,1)} %bitcast.20, ...), custom_call_target="tpu_custom_call" | custom-call | tf_op jit(solution)/shard_map/relay/pallas_call | solution.py:556
  80.7 3.2 %finish.1 = (bf16[128,2048]{1,0:T(8,128)(2,1)}, bf16[128,2048]{1,0:T(8,128)(2,1)}, f32[31,2,2048]{2,1,0:T(2,128)}, f32[2,2048]{1,0:T(2,128)}) custom-call(s32[1]{0:T(128)} %bitcast.section, s32[2,96]{1,0:T(2,128)} %bitcast.22, bf16[128,2048]{1,0:T(8,128)(2,1)} %get-tuple-element.11.act, bf16[128,2048]{1,0:T(8,128)(2,1)} %get-tuple-element.12.grad, ...), custom_call_target="tpu_custom_call" | custom-call | tf_op jit(solution)/shard_map/finish/pallas_call | solution.py:673

commit v3 on v2

--- a/solution.py
+++ b/solution.py
@@ -242,9 +242,6 @@
             m_ref,
         )
 
-    loads[0].wait()
-    loads[1].wait()
-    pick(2)
     pl.semaphore_wait(barrier, len(peers))
 
     halos = {}
@@ -256,11 +253,17 @@
                 launch(remote(ref.at[edge], hx.at[n, side], hx_s.at[n, side], hx_r.at[n, side], (s, peer)))
             )
 
+    loads[0].wait()
+    loads[1].wait()
+    pick(2)
     loads[2].wait()
     norm_own(x_b.at[0], b_len[0], 2, m_b.at[0], 0)
     loads[3].wait()
     pick(0)
     norm_own(x_f, f_len[0], 0, m_f)
+    loads[4].wait()
+    pick(3)
+    norm_own(x_b.at[1], b_len[1], 3, m_b.at[1], 1)
 
     def forward(tick, x_ref, dst):
         copies = [
@@ -469,14 +472,20 @@
     norm_edges(hx.at[1], b_len[0], 2, m_b.at[0])
     loads[5].wait()
 
-    @pl.loop(0, blocks)
-    def _(c):
-        total = conv_block(m_b.at[0], k_ref, 2, c, 0, 2 * tiles, False)
-        for r in range(tiles):
-            conv = jnp.concatenate(total[2 * r : 2 * r + 2], axis=0)
-            put_mixed(0, c, r, g_in[pl.ds(16 * r, 16), lanes_of(c)].astype(f32) * slope(conv))
-
-    mixed = send_mixed(0)
+    for segments in (outer, inner):
+
+        @pl.loop(0, blocks)
+        def _(c):
+            for first, groups in segments:
+                total = conv_block(m_b.at[0], k_ref, 2, c, first, groups, False)
+                for n in range(groups // 2):
+                    r = first // 2 + n
+                    conv = jnp.concatenate(total[2 * n : 2 * n + 2], axis=0)
+                    put_mixed(0, c, r, g_in[pl.ds(16 * r, 16), lanes_of(c)].astype(f32) * slope(conv))
+
+        if segments is outer:
+            mixed = send_mixed(0)
+
     for copy in halos[0]:
         copy.wait_recv()
     norm_edges(hx.at[0], f_len[0], 0, m_f)
@@ -490,9 +499,6 @@
     taps(0)
     scatter(0)
 
-    loads[4].wait()
-    pick(3)
-    norm_own(x_b.at[1], b_len[1], 3, m_b.at[1], 1)
     for copy in halos[2]:
         copy.wait_recv()
     norm_edges(hx.at[2], b_len[1], 3, m_b.at[1])
@@ -633,6 +639,9 @@
     bring.start()
     for come, _ in moves:
         come.start()
+    for come, go in moves:
+        come.wait()
+        go.start()
     bring.wait()
     full[...] = fin_v[...].astype(f32)
     slot = lax.broadcasted_iota(jnp.int32, (2, LANES), 0)
@@ -643,24 +652,19 @@
         lanes = pl.ds(c * LANES, LANES)
         return sum(hot[k] * jnp.broadcast_to(full[k, pl.ds(j, 1), lanes], (2, LANES)) for k in range(2))
 
+    put = []
+    for n, (first, count) in enumerate(((0, 8), (8, 8), (16, 8), (24, 7))):
+        for j in range(first, first + count):
+            for c in range(blocks):
+                taps[j, :, pl.ds(c * LANES, LANES)] = one(j, c)
+        at = pl.ds(first, count)
+        put.append(pltpu.make_async_copy(taps.at[at], tap_out.at[at], sem_out.at[4 + n]))
+        put[-1].start()
     for c in range(blocks):
         gains[:, pl.ds(c * LANES, LANES)] = one(31, c)
-
-    for j in range(31):
-        for c in range(blocks):
-            taps[j, :, pl.ds(c * LANES, LANES)] = one(j, c)
-
-    put = [
-        pltpu.make_async_copy(taps, tap_out, sem_out.at[4]),
-        pltpu.make_async_copy(gains, gain_out, sem_out.at[5]),
-    ]
-    for copy in put:
-        copy.start()
-    for come, go in moves:
-        come.wait()
-        go.start()
-        put.append(go)
-    for copy in put:
+    put.append(pltpu.make_async_copy(gains, gain_out, sem_out.at[8]))
+    put[-1].start()
+    for copy in put + [go for _, go in moves]:
         copy.wait()
 
 
@@ -687,7 +691,7 @@
             vm((31, 2, width), f32),
             vm((2, width), f32),
             dma((5,)),
-            dma((6,)),
+            dma((9,)),
         ],
         compiler_params=pltpu.CompilerParams(vmem_limit_bytes=56 << 20),
         name="finish",

time: 84.1 us -> 83.9 us (level)
  the two profiles are of different devices: /device:TPU:4 before, /device:TPU:8 now
where the time goes in v3:
time: 83.9 us; the launch traced here: 83.7 us
  Pallas kernels  83.1 us (99%)
    pallas_call x1, Pallas kernels, relay(): pl.pallas_call(functools.partial(body, sections, shards), out_shape=[jax....  80 us
    pallas_call x1, Pallas kernels, finish(): pl.pallas_call(finish_body, out_shape=[jax.ShapeDtypeStruct((rows, width)...  3.03 us

profile of v3, /device:TPU:8, one launch (start us, length us, event | category | flops | bytes accessed | tf_op | source)
XLA Modules:
  0.0 83.7 jit_solution(15968686089205059649)
XLA Ops:
  0.6 80.0 %relay.1 = (bf16[128,2048]{1,0:T(8,128)(2,1)}, bf16[128,2048]{1,0:T(8,128)(2,1)}, bf16[2,32,2048]{2,1,0:T(8,128)(2,1)}) custom-call(bf16[128,2048]{1,0:T(8,128)(2,1)} %bitcast.17, bf16[128,2048]{1,0:T(8,128)(2,1)} %bitcast.18, bf16[2,128,2048]{2,1,0:T(8,128)(2,1)} %bitcast.16, bf16[31,2,2048]{2,1,0:T(2,128)(2,1)} %bitcast.19, bf16[2,2048]{1,0:T(2,128)(2,1)} %bitcast.20, ...), custom_call_target="tpu_custom_call" | custom-call | tf_op jit(solution)/shard_map/relay/pallas_call | solution.py:562
  80.7 3.0 %finish.1 = (bf16[128,2048]{1,0:T(8,128)(2,1)}, bf16[128,2048]{1,0:T(8,128)(2,1)}, f32[31,2,2048]{2,1,0:T(2,128)}, f32[2,2048]{1,0:T(2,128)}) custom-call(s32[1]{0:T(128)} %bitcast.section, s32[2,96]{1,0:T(2,128)} %bitcast.22, bf16[128,2048]{1,0:T(8,128)(2,1)} %get-tuple-element.11.act, bf16[128,2048]{1,0:T(8,128)(2,1)} %get-tuple-element.12.grad, ...), custom_call_target="tpu_custom_call" | custom-call | tf_op jit(solution)/shard_map/finish/pallas_call | solution.py:677
